TPU v7x, 32 devices: a whole 2x2x4 slice. The times are simulated.
32 devices in a mesh: wide: 8 (over z, y), narrow: 4 (over x, core).
Axes of the slice: x: 2, y: 2, z: 4, core: 2. Of those that a mesh axis runs over, the one named last changes fastest.
Arguments:
- entry_factor: bfloat16 [288, 4, 64, 1024], P('wide', 'narrow'), may hold values from -6 to 6
- entry_panel: int32 [288, 4], P('wide', 'narrow'), may hold values from 0 to 1
- entry_target: int32 [288, 4], P('wide', 'narrow'), may hold values from 0 to 7, as said below
- entry_count: int32 [4, 8], P('narrow', 'wide'), may hold values from 1 to 36, 96 in all within a row
- panel_shared: bfloat16 [16, 64, 1024], P('wide', None, 'narrow'), may hold values from -0.1875 to 0.1875
- coupling: float32 [16, 64, 64], P('wide'), may hold values from -0.75 to 0.75
- probes: bfloat16 [32, 64, 1024], P('narrow'), may hold values from -6 to 6
Outputs:
- left_factor: float32 [32, 64, 1024], P('narrow', None, 'wide')
- right_factor: float32 [32, 64, 1024], P('narrow', None, 'wide')
Inputs may be any that keep to these rules, and one draw needn't show every extreme that they name: `entry_panel`: the local panel of an entry of any slot, live or not. `entry_target`: the local target of an entry; every target has at least one live entry. `entry_count`: the live slots of one device; for every owner the counts over the 8 wide indices sum to 96, and some device holds exactly 36.
All inputs are finite; a program needn't handle non-finite values.
Results may differ from a plain program's by a relative error of at most 0.0036.
Values may be sent and summed in bfloat16 or wider, within the bound.
A program may use at most 64 MiB of HBM per device.

v0:
```python
import math
import jax
import jax.numpy as jnp
from jax import lax
from jax.sharding import PartitionSpec as P


def wide_reduce(x, count):
    lead, rows, width = x.shape
    pieces = x.reshape(lead, rows, count, width // count).transpose(2, 0, 1, 3)
    pieces = lax.all_to_all(pieces, "wide", 0, 0, tiled=True)
    return pieces.sum(axis=0)


def wide_gather(x, count):
    lead, rows, width = x.shape
    copies = jnp.broadcast_to(x[None], (count, lead, rows, width))
    copies = lax.all_to_all(copies, "wide", 0, 0, tiled=True)
    return copies.transpose(1, 2, 0, 3).reshape(lead, rows, count * width)


def lower_inverse(lower):
    highest = lax.Precision.HIGHEST
    size = lower.shape[-1]
    eye = jnp.eye(size, dtype=lower.dtype)
    diag = jnp.diagonal(lower, axis1=-2, axis2=-1)
    strict = eye - lower / diag[..., :, None]
    unit_inverse = eye + strict
    power = strict
    for _ in range(max(size - 1, 1).bit_length() - 1):
        power = jnp.einsum("tij,tjk->tik", power, power, precision=highest)
        unit_inverse = unit_inverse + jnp.einsum(
            "tij,tjk->tik", unit_inverse, power, precision=highest
        )
    return unit_inverse / diag[..., None, :]


def shards(entry_factor, entry_panel, entry_target, entry_count, panel_shared, coupling, probes):
    highest = lax.Precision.HIGHEST
    factors = entry_factor[:, 0]
    slot_count = factors.shape[0]
    rank_dim = factors.shape[1]
    full_width = factors.shape[2]
    panel_count = panel_shared.shape[0]
    target_count = probes.shape[0]
    live_mask = (jnp.arange(slot_count) < entry_count[0, 0]).astype(jnp.float32)
    pick_panel = (entry_panel == jnp.arange(panel_count)[None, :]).astype(jnp.float32) * live_mask[
        :, None
    ]
    pick_target = (entry_target == jnp.arange(target_count)[None, :]).astype(jnp.float32)
    pair_pick = (pick_panel[:, :, None] * pick_target[:, None, :]).reshape(
        slot_count, panel_count * target_count
    )
    gathered = lax.all_gather(panel_shared, "narrow", axis=2, tiled=True)
    projected = jnp.einsum("drb,tkb->dtrk", gathered, probes, preferred_element_type=jnp.float32)
    coefficients = jnp.einsum("dij,dtjk->dtik", coupling, projected, precision=highest).astype(
        jnp.bfloat16
    )
    coeff_table = coefficients.reshape(panel_count * target_count, rank_dim * rank_dim)
    chosen = jnp.dot(
        pair_pick.astype(jnp.bfloat16), coeff_table, preferred_element_type=jnp.float32
    )
    chosen = chosen.astype(jnp.bfloat16).reshape(slot_count, rank_dim, rank_dim)
    contributions = jnp.einsum("eji,ejb->eib", chosen, factors, preferred_element_type=jnp.float32)
    sketch = jnp.einsum("et,eib->tib", pick_target, contributions, precision=highest)
    wide_count = lax.axis_size("wide")
    share_cols = full_width // wide_count
    sketch_own = wide_reduce(sketch, wide_count)
    gram_part = jnp.einsum("tib,tjb->tij", sketch_own, sketch_own, precision=highest)
    gram_copies = jnp.broadcast_to(gram_part[None], (wide_count,) + gram_part.shape)
    gram_matrix = lax.all_to_all(gram_copies, "wide", 0, 0, tiled=True).sum(axis=0)
    sketch_sum = wide_gather(sketch_own, wide_count)
    lower_factor = jnp.linalg.cholesky(gram_matrix)
    basis = jnp.einsum("tij,tjb->tib", lower_inverse(lower_factor), sketch_sum, precision=highest)
    basis_round = basis.astype(jnp.bfloat16)
    own_basis = lax.dynamic_slice_in_dim(basis, lax.axis_index("wide") * share_cols, share_cols, 2)
    selected = jnp.einsum(
        "et,tkb->ekb",
        pick_target.astype(jnp.bfloat16),
        basis_round,
        preferred_element_type=jnp.float32,
    )
    selected = selected.astype(jnp.bfloat16)
    back_terms = jnp.einsum("eib,ekb->eik", factors, selected, preferred_element_type=jnp.float32)
    summed = jnp.einsum("ep,eik->pik", pair_pick, back_terms, precision=highest)
    summed = summed.reshape(panel_count, target_count, rank_dim, rank_dim)
    middle_terms = jnp.einsum("dtik,dij->dtkj", summed, coupling, precision=highest)
    partial_rows = jnp.einsum(
        "dtkj,djb->tkb", middle_terms, gathered.astype(jnp.float32), precision=highest
    )
    coeff_part = wide_reduce(partial_rows, wide_count)
    root_width = math.sqrt(full_width)
    return (own_basis * root_width, coeff_part / root_width)


def solution(mesh):
    placed = (
        P("wide", "narrow", None, None),
        P("wide", "narrow"),
        P("wide", "narrow"),
        P("narrow", "wide"),
        P("wide", None, "narrow"),
        P("wide", None, None),
        P("narrow", None, None),
    )
    return jax.shard_map(
        shards,
        mesh=mesh,
        in_specs=placed,
        out_specs=(P("narrow", None, "wide"), P("narrow", None, "wide")),
        check_vma=False,
    )
```

profile of v0, /device:TPU:0, one launch (start us, length us, event | category | flops | bytes accessed | tf_op | source)
XLA Modules:
  0.0 250.5 jit_solution(6765023599289800090)
XLA Ops:
  0.7 0.7 fusion.42
  1.4 7.4 %all_gather.3 = bf16[2,64,1024]{2,1,0:T(8,128)(2,1)S(1)} all-gather(bf16[2,64,256]{2,1,0:T(8,128)(2,1)} %param.11), channel_id=1, replica_groups=mesh['wide'=8,'narrow'=4] {'narrow'}, dimensions={2}, use_global_device_ids=true | all-gather | bytes 327680 | tf_op jit(solution)/shard_map/all_gather | solution.py:54
  8.8 0.5 convolution_bitcast_fusion.1
  9.3 0.2 copy-done.1
  9.5 0.6 fusion.20
  10.1 0.2 copy.37
  10.3 0.3 reshape.113
  11.3 0.3 convolution_convert_fusion
  11.6 0.6 reshape.114
  12.2 3.8 %fusion.4 = f32[36,64,1024]{2,1,0:T(8,128)S(1)} fusion(bf16[36,64,64]{2,1,0:T(8,128)(2,1)S(1)} %reshape.114, bf16[36,1,64,1024]{3,2,1,0:T(8,128)(2,1)} %param.7), kind=kOutput, calls=%fused_computation.5 | convolution fusion | flops 301989888 | bytes 14450688 | tf_op jit(solution)/shard_map/eji,ejb->eib/dot_general | solution.py:64
  16.0 8.9 %fusion.10 = f32[8,64,8,128]{3,0,2,1:T(8,128)S(1)} fusion(f32[36,64,1024]{2,1,0:T(8,128)S(1)} %fusion.4, s32[36]{0:T(128)S(1)} %bitcast.117), kind=kOutput, calls=%fused_computation.15 | convolution fusion | flops 226492704 | bytes 11534480 | tf_op jit(solution)/shard_map/et,eib->tib/dot_general | solution.py:65
  25.0 54.4 %all_to_all.20 = f32[8,8,64,128]{3,1,2,0:T(8,128)S(1)} all-to-all(f32[8,8,64,128]{3,1,2,0:T(8,128)S(1)} %bitcast.114), channel_id=1, replica_groups=mesh['wide'=8,'narrow'=4] {'wide'}, dimensions={0} | all-to-all | bytes 4194304 | tf_op jit(solution)/shard_map/all_to_all | solution.py:11
  79.5 0.5 fusion.48
  80.1 0.2 broadcast_in_dim.11
  80.3 2.1 reshape.132
  82.5 3.6 %all-to-all-start.1 = ((f32[8,1,32768]{2,1,0:T(1,128)}), f32[8,1,32768]{2,1,0:T(1,128)S(1)}, u32[]{:S(2)}, u32[]{:S(2)}) async-start(f32[8,1,32768]{2,1,0:T(1,128)} %reshape.132), calls=%async_computation.1 | async-start | bytes 2097152 | tf_op jit(solution)/shard_map/all_to_all | solution.py:71
  86.2 25.8 %all-to-all-done.1 = f32[8,1,32768]{2,1,0:T(1,128)S(1)} async-done(((f32[8,1,32768]{2,1,0:T(1,128)}), f32[8,1,32768]{2,1,0:T(1,128)S(1)}, u32[]{:S(2)}, u32[]{:S(2)}) %all-to-all-start.1) | async-done | bytes 1048608 | tf_op jit(solution)/shard_map/all_to_all | solution.py:71
  112.0 1.6 broadcast_in_dim.12
  113.5 4.3 %all-to-all-start.2 = ((f32[8,8,64,128]{3,2,1,0:T(8,128)}), f32[8,8,64,128]{3,2,1,0:T(8,128)}, u32[]{:S(2)}, u32[]{:S(2)}) async-start(f32[8,8,64,128]{3,2,1,0:T(8,128)} %broadcast_in_dim.12), calls=%async_computation.2 | async-start | bytes 4194304 | tf_op jit(solution)/shard_map/all_to_all | solution.py:18
  117.9 0.5 broadcast.125
  118.4 4.5 %reduce.6 = f32[8,32768]{1,0:T(8,128)} reduce(f32[8,1,32768]{2,1,0:T(1,128)S(1)} %all-to-all-done.1, f32[]{:T(128)} %broadcast.125), dimensions={1}, to_apply=%all_to_all.13.reduce_sub_computation | reduce | bytes 2097156 | tf_op jit(solution)/shard_map/all_to_all | solution.py:71
  122.9 2.1 reshape.133
  125.0 0.2 reduce_sum.28
  125.4 47.1 %custom-call.4 = f32[8,64,64]{2,1,0:T(8,128)S(1)} custom-call(f32[8,64,64]{2,1,0:T(8,128)S(1)} %fusion.27), custom_call_target="Cholesky" | custom-call | tf_op jit(solution)/shard_map/jit(cholesky)/cholesky | solution.py:73
  172.8 0.6 copy.45
  173.4 0.9 gather_fusion
  174.4 0.5 fusion.31
  174.9 0.4 fusion.51
  175.3 0.4 fusion.52
  175.7 0.5 convolution_add_fusion.4
  176.2 0.4 convolution_add_fusion.3
  176.6 0.4 fusion.53
  177.0 0.4 convolution_add_fusion.2
  177.4 0.4 fusion.54
  177.8 0.4 convolution_add_fusion.1
  178.2 0.4 fusion.21
  178.6 4.7 %fusion.50 = (bf16[8,64,1024]{2,1,0:T(8,128)(2,1)S(1)}, f32[8,64,1024]{2,1,0:T(8,128)}) fusion(f32[8,64,64]{2,1,0:T(8,128)S(1)} %fusion.21, f32[8,8,64,128]{3,2,1,0:T(8,128)} %all-to-all-done.2), kind=kOutput, calls=%fused_computation.69 | convolution fusion | flops 403177472 | bytes 5373952 | tf_op jit(solution)/shard_map/tij,tjb->tib/dot_general | solution.py:74
  183.3 1.6 convolution_convert_fusion.1
  184.9 5.5 %fusion.13 = f32[36,64,64]{1,2,0:T(8,128)S(1)} fusion(bf16[36,1,64,1024]{3,2,1,0:T(8,128)(2,1)} %param.7, bf16[36,64,1024]{2,0,1:T(8,128)(2,1)S(1)} %convolution_convert_fusion.1), kind=kOutput, calls=%fused_computation.17 | convolution fusion | flops 301989888 | bytes 10027008 | tf_op jit(solution)/shard_map/eib,ekb->eik/dot_general | solution.py:84
  190.4 0.5 copy.52
  190.9 1.0 fusion.18
  191.9 1.8 fusion.24
  193.8 1.0 convolution_bitcast_fusion
  194.8 1.6 copy.85
  196.4 5.9 %all-to-all-start.3 = ((f32[8,8,64,128]{3,2,1,0:T(8,128)}), f32[8,8,64,128]{3,2,1,0:T(8,128)S(1)}, u32[]{:S(2)}, u32[]{:S(2)}) async-start(f32[8,8,64,128]{3,2,1,0:T(8,128)} %bitcast.113), calls=%async_computation.3 | async-start | bytes 4194304 | tf_op jit(solution)/shard_map/all_to_all | solution.py:11
  202.4 1.7 dynamic-slice_multiply_fusion
  204.0 45.6 %all-to-all-done.3 = f32[8,8,64,128]{3,2,1,0:T(8,128)S(1)} async-done(((f32[8,8,64,128]{3,2,1,0:T(8,128)}), f32[8,8,64,128]{3,2,1,0:T(8,128)S(1)}, u32[]{:S(2)}, u32[]{:S(2)}) %all-to-all-start.3) | async-done | bytes 2097184 | tf_op jit(solution)/shard_map/all_to_all | solution.py:11
  249.7 0.7 broadcast_multiply_fusion
  (28 shorter events, 1.0 us)
Async XLA Ops:
  0.6 8.2 %copy-start = (bf16[8,64,1024]{2,1,0:T(8,128)(2,1)S(1)}, bf16[8,64,1024]{2,1,0:T(8,128)(2,1)}, u32[]{:S(2)}) copy-start(bf16[8,64,1024]{2,1,0:T(8,128)(2,1)} %param.13) | copy-start | bytes 3145732
  0.6 8.9 %copy-start.3 = (f32[2,64,64]{2,1,0:T(8,128)S(1)}, f32[2,64,64]{2,1,0:T(8,128)}, u32[]{:S(2)}) copy-start(f32[2,64,64]{2,1,0:T(8,128)} %param.12) | copy-start | bytes 98308
  0.7 10.6 %copy-start.5 = (s32[36,1]{0,1:T(1,128)S(1)}, s32[36,1]{0,1:T(1,128)}, u32[]{:S(2)}) copy-start(s32[36,1]{0,1:T(1,128)} %param.8) | copy-start | bytes 436
  8.8 0.7 copy-start.1
  12.2 3.8 %copy-start.4 = (s32[36,1]{0,1:T(1,128)S(1)}, s32[36,1]{0,1:T(1,128)}, u32[]{:S(2)}) copy-start(s32[36,1]{0,1:T(1,128)} %param.9) | copy-start | bytes 436
  82.5 29.5 %all-to-all-start.1 = ((f32[8,1,32768]{2,1,0:T(1,128)}), f32[8,1,32768]{2,1,0:T(1,128)S(1)}, u32[]{:S(2)}, u32[]{:S(2)}) async-start(f32[8,1,32768]{2,1,0:T(1,128)} %reshape.132), calls=%async_computation.1 | async-start | bytes 2097152 | tf_op jit(solution)/shard_map/all_to_all | solution.py:71
  113.5 65.1 %all-to-all-start.2 = ((f32[8,8,64,128]{3,2,1,0:T(8,128)}), f32[8,8,64,128]{3,2,1,0:T(8,128)}, u32[]{:S(2)}, u32[]{:S(2)}) async-start(f32[8,8,64,128]{3,2,1,0:T(8,128)} %broadcast_in_dim.12), calls=%async_computation.2 | async-start | bytes 4194304 | tf_op jit(solution)/shard_map/all_to_all | solution.py:18
  190.9 2.9 %copy-start.2 = (bf16[2,64,1024]{2,1,0:T(8,128)(2,1)S(1)}, bf16[2,64,1024]{2,1,0:T(8,128)(2,1)}, u32[]{:S(2)}) copy-start(bf16[2,64,1024]{2,1,0:T(8,128)(2,1)} %copy-done.1) | copy-start | bytes 786436
  196.4 53.1 %all-to-all-start.3 = ((f32[8,8,64,128]{3,2,1,0:T(8,128)}), f32[8,8,64,128]{3,2,1,0:T(8,128)S(1)}, u32[]{:S(2)}, u32[]{:S(2)}) async-start(f32[8,8,64,128]{3,2,1,0:T(8,128)} %bitcast.113), calls=%async_computation.3 | async-start | bytes 4194304 | tf_op jit(solution)/shard_map/all_to_all | solution.py:11
where the time goes:
time: 251 us; the launch traced here: 250 us
  waiting for transfers between devices  71.4 us (28%)
  blocking collectives  61.8 us (25%)
  other arithmetic  55.6 us (22%)
  matrix products  34.3 us (14%)
  starting transfers between devices  13.9 us (6%)
  local copies, waits for them, and re-layouts  11.9 us (5%)
    all_to_all x1, blocking collectives, wide_reduce(): pieces = lax.all_to_all(pieces, 'wide', 0, 0, tiled=True)  54.4 us
    another operation x3, other arithmetic, shards(): lower_factor = jnp.linalg.cholesky(gram_matrix)  47.3 us
    all_to_all x1, waiting for transfers between devices, wide_reduce(): pieces = lax.all_to_all(pieces, 'wide', 0, 0, tiled=True)  45.6 us
    all_to_all x1, waiting for transfers between devices, shards(): lax.all_to_all(gram_copies, 'wide', 0, 0, tiled=True).sum(axis=0)  25.8 us
    dot_general x1, matrix products, shards(): jnp.einsum('et,eib->tib', pick_target, contributions, precision=highest)  8.9 us
    all_gather x1, blocking collectives, shards(): gathered = lax.all_gather(panel_shared, 'narrow', axis=2, tiled=True)  7.42 us
    all_to_all x1, starting transfers between devices, wide_reduce(): pieces = lax.all_to_all(pieces, 'wide', 0, 0, tiled=True)  5.91 us
    dot_general x1, matrix products, shards(): jnp.einsum('eib,ekb->eik', factors, selected, preferred_element_type=jnp....  5.48 us
  transfers between devices with their start and end apart: 3, of which 2 were waited for; matrix products, arithmetic and copies ran while one was open for 25% of the time, Pallas kernels for 0%

commit v1 on v0

--- a/solution.py
+++ b/solution.py
@@ -51,7 +51,15 @@
     pair_pick = (pick_panel[:, :, None] * pick_target[:, None, :]).reshape(
         slot_count, panel_count * target_count
     )
-    gathered = lax.all_gather(panel_shared, "narrow", axis=2, tiled=True)
+    ways, here, step = (lax.axis_size("narrow"), lax.axis_index("narrow"), panel_shared.shape[2])
+    line, have = (panel_shared, 1)
+    while have < ways:
+        line = jnp.concatenate(
+            [line, lax.ppermute(line, "narrow", [(d, (d - have) % ways) for d in range(ways)])],
+            axis=2,
+        )
+        have = 2 * have
+    gathered = jnp.roll(line, here * step, axis=2)
     projected = jnp.einsum("drb,tkb->dtrk", gathered, probes, preferred_element_type=jnp.float32)
     coefficients = jnp.einsum("dij,dtjk->dtik", coupling, projected, precision=highest).astype(
         jnp.bfloat16

time: 251 us -> 255 us (1.016)
  blocking collectives: 61.8 us -> 53.8 us
  waiting for transfers between devices: 71.4 us -> 75.7 us
  starting transfers between devices: 13.9 us -> 16.9 us
    all_gather x1 -> x0, blocking collectives: 7.42 us -> none  [shards(): gathered = lax.all_gather(panel_shared, 'narrow', axis=2, tiled=True)]
    ppermute x0 -> x2, waiting for transfers between devices: none -> 4.84 us  [shards(): lax.ppermute(line, 'narrow', [(d, (d - have) % ways) for d in range(ways)])]
    ppermute x0 -> x2, starting transfers between devices: none -> 3.09 us  [shards(): lax.ppermute(line, 'narrow', [(d, (d - have) % ways) for d in range(ways)])]
    unnamed x14 -> x17, local copies, waits for them, and re-layouts: 4.46 us -> 6.74 us
  transfers between devices with their start and end apart: 3 -> 5, of which waited for: 2 -> 4; matrix products, arithmetic and copies ran while one was open for 25% -> 25% of each run, Pallas kernels for 0% -> 0%
where the time goes in v1:
time: 255 us; the launch traced here: 254 us
  waiting for transfers between devices  75.7 us (30%)
  other arithmetic  57 us (22%)
  blocking collectives  53.8 us (21%)
  matrix products  35 us (14%)
  starting transfers between devices  16.9 us (7%)
  local copies, waits for them, and re-layouts  14.1 us (6%)
    all_to_all x1, blocking collectives, wide_reduce(): pieces = lax.all_to_all(pieces, 'wide', 0, 0, tiled=True)  53.8 us
    another operation x3, other arithmetic, shards(): lower_factor = jnp.linalg.cholesky(gram_matrix)  47.3 us
    all_to_all x1, waiting for transfers between devices, wide_reduce(): pieces = lax.all_to_all(pieces, 'wide', 0, 0, tiled=True)  45.4 us
    all_to_all x1, waiting for transfers between devices, shards(): lax.all_to_all(gram_copies, 'wide', 0, 0, tiled=True).sum(axis=0)  25.5 us
    dot_general x1, matrix products, shards(): jnp.einsum('et,eib->tib', pick_target, contributions, precision=highest)  8.9 us
    unnamed x17, local copies, waits for them, and re-layouts  6.74 us
    all_to_all x1, starting transfers between devices, wide_reduce(): pieces = lax.all_to_all(pieces, 'wide', 0, 0, tiled=True)  5.9 us
    dot_general x1, matrix products, shards(): jnp.einsum('eib,ekb->eik', factors, selected, preferred_element_type=jnp....  5.48 us
  transfers between devices with their start and end apart: 5, of which 4 were waited for; matrix products, arithmetic and copies ran while one was open for 25% of the time, Pallas kernels for 0%

profile of v1, /device:TPU:0, one launch (start us, length us, event | category | flops | bytes accessed | tf_op | source)
XLA Modules:
  0.0 254.2 jit_solution(18062857953686306918)
XLA Ops:
  0.7 2.5 collective-permute-start
  3.1 0.7 fusion.44
  4.4 0.7 compare_select_fusion
  5.3 0.8 pad_maximum_fusion
  6.2 0.6 collective-permute-start.1
  6.8 0.8 constant_dynamic-update-slice_fusion.5
  7.7 4.6 %collective-permute-done.1 = bf16[2,64,512]{2,1,0:T(8,128)(2,1)S(1)} collective-permute-done((bf16[2,64,512]{2,1,0:T(8,128)(2,1)S(1)}, bf16[2,64,512]{2,1,0:T(8,128)(2,1)S(1)}, u32[]{:S(2)}, u32[]{:S(2)}) %collective-permute-start.1) | collective-permute-done | bytes 131104 | tf_op jit(solution)/shard_map/ppermute | solution.py:58
  12.3 0.8 constant_dynamic-update-slice_fusion.2
  13.2 0.8 copy-done.1
  14.0 0.7 convolution_bitcast_fusion.1
  14.7 1.0 fusion.20
  16.4 0.6 reshape.114
  17.1 3.8 %fusion.4 = f32[36,64,1024]{2,1,0:T(8,128)S(1)} fusion(bf16[36,64,64]{2,1,0:T(8,128)(2,1)S(1)} %reshape.114, bf16[36,1,64,1024]{3,2,1,0:T(8,128)(2,1)} %param.7), kind=kOutput, calls=%fused_computation.5 | convolution fusion | flops 301989888 | bytes 14450688 | tf_op jit(solution)/shard_map/eji,ejb->eib/dot_general | solution.py:72
  20.8 8.9 %fusion.10 = f32[8,64,8,128]{3,0,2,1:T(8,128)S(1)} fusion(f32[36,64,1024]{2,1,0:T(8,128)S(1)} %fusion.4, s32[36]{0:T(128)S(1)} %bitcast.117), kind=kOutput, calls=%fused_computation.15 | convolution fusion | flops 226492704 | bytes 11534480 | tf_op jit(solution)/shard_map/et,eib->tib/dot_general | solution.py:73
  29.9 53.8 %all_to_all.20 = f32[8,8,64,128]{3,1,2,0:T(8,128)S(1)} all-to-all(f32[8,8,64,128]{3,1,2,0:T(8,128)S(1)} %bitcast.114), channel_id=1, replica_groups=mesh['wide'=8,'narrow'=4] {'wide'}, dimensions={0} | all-to-all | bytes 4194304 | tf_op jit(solution)/shard_map/all_to_all | solution.py:11
  83.8 0.5 fusion.52
  84.6 2.1 reshape.132
  86.7 3.6 %all-to-all-start.1 = ((f32[8,1,32768]{2,1,0:T(1,128)}), f32[8,1,32768]{2,1,0:T(1,128)S(1)}, u32[]{:S(2)}, u32[]{:S(2)}) async-start(f32[8,1,32768]{2,1,0:T(1,128)} %reshape.132), calls=%async_computation.1 | async-start | bytes 2097152 | tf_op jit(solution)/shard_map/all_to_all | solution.py:79
  90.4 25.5 %all-to-all-done.1 = f32[8,1,32768]{2,1,0:T(1,128)S(1)} async-done(((f32[8,1,32768]{2,1,0:T(1,128)}), f32[8,1,32768]{2,1,0:T(1,128)S(1)}, u32[]{:S(2)}, u32[]{:S(2)}) %all-to-all-start.1) | async-done | bytes 1048608 | tf_op jit(solution)/shard_map/all_to_all | solution.py:79
  115.9 1.6 broadcast_in_dim.12
  117.4 4.3 %all-to-all-start.2 = ((f32[8,8,64,128]{3,2,1,0:T(8,128)}), f32[8,8,64,128]{3,2,1,0:T(8,128)}, u32[]{:S(2)}, u32[]{:S(2)}) async-start(f32[8,8,64,128]{3,2,1,0:T(8,128)} %broadcast_in_dim.12), calls=%async_computation.2 | async-start | bytes 4194304 | tf_op jit(solution)/shard_map/all_to_all | solution.py:18
  121.8 0.5 broadcast.126
  122.4 4.5 %reduce.6 = f32[8,32768]{1,0:T(8,128)} reduce(f32[8,1,32768]{2,1,0:T(1,128)S(1)} %all-to-all-done.1, f32[]{:T(128)} %broadcast.126), dimensions={1}, to_apply=%all_to_all.13.reduce_sub_computation | reduce | bytes 2097156 | tf_op jit(solution)/shard_map/all_to_all | solution.py:79
  126.9 2.1 reshape.133
  129.3 47.1 %custom-call.4 = f32[8,64,64]{2,1,0:T(8,128)S(1)} custom-call(f32[8,64,64]{2,1,0:T(8,128)S(1)} %fusion.27), custom_call_target="Cholesky" | custom-call | tf_op jit(solution)/shard_map/jit(cholesky)/cholesky | solution.py:81
  176.7 0.6 copy.47
  177.4 0.9 gather_fusion
  178.3 0.5 fusion.33
  178.8 0.4 fusion.55
  179.6 0.5 convolution_add_fusion.4
  180.1 0.4 convolution_add_fusion.3
  180.5 0.4 fusion.57
  180.9 0.4 convolution_add_fusion.2
  181.3 0.4 fusion.58
  181.7 0.4 convolution_add_fusion.1
  182.1 0.4 fusion.21
  182.5 4.7 %fusion.54 = (bf16[8,64,1024]{2,1,0:T(8,128)(2,1)S(1)}, f32[8,64,1024]{2,1,0:T(8,128)}) fusion(f32[8,64,64]{2,1,0:T(8,128)S(1)} %fusion.21, f32[8,8,64,128]{3,2,1,0:T(8,128)} %all-to-all-done.2), kind=kOutput, calls=%fused_computation.80 | convolution fusion | flops 403177472 | bytes 5373952 | tf_op jit(solution)/shard_map/tij,tjb->tib/dot_general | solution.py:82
  187.3 1.6 convolution_convert_fusion.1
  188.8 5.5 %fusion.13 = f32[36,64,64]{1,2,0:T(8,128)S(1)} fusion(bf16[36,1,64,1024]{3,2,1,0:T(8,128)(2,1)} %param.7, bf16[36,64,1024]{2,0,1:T(8,128)(2,1)S(1)} %convolution_convert_fusion.1), kind=kOutput, calls=%fused_computation.17 | convolution fusion | flops 301989888 | bytes 10027008 | tf_op jit(solution)/shard_map/eib,ekb->eik/dot_general | solution.py:92
  194.3 0.5 copy.54
  194.8 1.0 fusion.18
  195.9 1.8 fusion.24
  197.7 1.0 convolution_bitcast_fusion
  198.7 1.6 copy.88
  200.4 5.9 %all-to-all-start.3 = ((f32[8,8,64,128]{3,2,1,0:T(8,128)}), f32[8,8,64,128]{3,2,1,0:T(8,128)S(1)}, u32[]{:S(2)}, u32[]{:S(2)}) async-start(f32[8,8,64,128]{3,2,1,0:T(8,128)} %bitcast.113), calls=%async_computation.3 | async-start | bytes 4194304 | tf_op jit(solution)/shard_map/all_to_all | solution.py:11
  206.3 1.7 dynamic-slice_multiply_fusion
  208.0 45.4 %all-to-all-done.3 = f32[8,8,64,128]{3,2,1,0:T(8,128)S(1)} async-done(((f32[8,8,64,128]{3,2,1,0:T(8,128)}), f32[8,8,64,128]{3,2,1,0:T(8,128)S(1)}, u32[]{:S(2)}, u32[]{:S(2)}) %all-to-all-start.3) | async-done | bytes 2097184 | tf_op jit(solution)/shard_map/all_to_all | solution.py:11
  253.5 0.7 broadcast_multiply_fusion
  (36 shorter events, 2.8 us)
Async XLA Ops:
  0.6 13.3 %copy-start = (bf16[8,64,1024]{2,1,0:T(8,128)(2,1)S(1)}, bf16[8,64,1024]{2,1,0:T(8,128)(2,1)}, u32[]{:S(2)}) copy-start(bf16[8,64,1024]{2,1,0:T(8,128)(2,1)} %param.13) | copy-start | bytes 3145732
  0.6 14.0 %copy-start.3 = (f32[2,64,64]{2,1,0:T(8,128)S(1)}, f32[2,64,64]{2,1,0:T(8,128)}, u32[]{:S(2)}) copy-start(f32[2,64,64]{2,1,0:T(8,128)} %param.12) | copy-start | bytes 98308
  0.7 4.7 %collective-permute-start = (bf16[2,64,256]{2,1,0:T(8,128)(2,1)}, bf16[2,64,256]{2,1,0:T(8,128)(2,1)S(1)}, u32[]{:S(2)}, u32[]{:S(2)}) collective-permute-start(bf16[2,64,256]{2,1,0:T(8,128)(2,1)} %param.11), channel_id=1, source_target_pairs={{0,3},{1,0},{2,1},{3,2},{4,7},{5,4},{6,5},{7,6},{8,11},{9,8},{10,9... | collective-permute-start | bytes 196616 | tf_op jit(solution)/shard_map/ppermute | solution.py:58
  6.2 6.1 %collective-permute-start.1 = (bf16[2,64,512]{2,1,0:T(8,128)(2,1)S(1)}, bf16[2,64,512]{2,1,0:T(8,128)(2,1)S(1)}, u32[]{:S(2)}, u32[]{:S(2)}) collective-permute-start(bf16[2,64,512]{2,1,0:T(8,128)(2,1)S(1)} %pad_maximum_fusion), channel_id=1, source_target_pairs={{0,2},{1,3},{2,0},{3,1},{4,6},{5,7},{6,4},{7,5},{8,10},{9,11},{10,... | collective-permute-start | bytes 393224 | tf_op jit(solution)/shard_map/ppermute | solution.py:58
  13.2 0.8 copy-start.1
  17.0 3.8 %copy-start.4 = (s32[36,1]{0,1:T(1,128)S(1)}, s32[36,1]{0,1:T(1,128)}, u32[]{:S(2)}) copy-start(s32[36,1]{0,1:T(1,128)} %param.9) | copy-start | bytes 436
  86.7 29.2 %all-to-all-start.1 = ((f32[8,1,32768]{2,1,0:T(1,128)}), f32[8,1,32768]{2,1,0:T(1,128)S(1)}, u32[]{:S(2)}, u32[]{:S(2)}) async-start(f32[8,1,32768]{2,1,0:T(1,128)} %reshape.132), calls=%async_computation.1 | async-start | bytes 2097152 | tf_op jit(solution)/shard_map/all_to_all | solution.py:79
  117.4 65.1 %all-to-all-start.2 = ((f32[8,8,64,128]{3,2,1,0:T(8,128)}), f32[8,8,64,128]{3,2,1,0:T(8,128)}, u32[]{:S(2)}, u32[]{:S(2)}) async-start(f32[8,8,64,128]{3,2,1,0:T(8,128)} %broadcast_in_dim.12), calls=%async_computation.2 | async-start | bytes 4194304 | tf_op jit(solution)/shard_map/all_to_all | solution.py:18
  194.8 2.9 %copy-start.2 = (bf16[2,64,2048]{2,1,0:T(8,128)(2,1)S(1)}, bf16[2,64,2048]{2,1,0:T(8,128)(2,1)}, u32[]{:S(2)}) copy-start(bf16[2,64,2048]{2,1,0:T(8,128)(2,1)} %copy-done.1) | copy-start | bytes 1572868
  200.4 52.9 %all-to-all-start.3 = ((f32[8,8,64,128]{3,2,1,0:T(8,128)}), f32[8,8,64,128]{3,2,1,0:T(8,128)S(1)}, u32[]{:S(2)}, u32[]{:S(2)}) async-start(f32[8,8,64,128]{3,2,1,0:T(8,128)} %bitcast.113), calls=%async_computation.3 | async-start | bytes 4194304 | tf_op jit(solution)/shard_map/all_to_all | solution.py:11
